TPU v7x, 128 devices: a whole 4x4x4 slice. The times are simulated.
128 devices in a mesh: req: 16 (over z, x_hi, core), mdl: 8 (over x_lo, y).
Axes of the slice: x: 4 (x_hi: 2, x_lo: 2; x = x_hi * 2 + x_lo), y: 4, z: 4, core: 2. Of those that a mesh axis runs over, the one named last changes fastest.
Arguments:
- tokens: bfloat16 [16384, 2048], P('req'), may hold values from -6 to 6
- doc_ids: int32 [16384], P('req'), may hold values from 0 to 16383, as said below
- positions: int32 [16384], P('req'), may hold values from 0 to 1023, as said below
- attn_gain: float32 [2048], replicated, may hold values from 0.5 to 1.5
- mlp_gain: float32 [2048], replicated, may hold values from 0.5 to 1.5
- q_gain: float32 [128], replicated, may hold values from 0.5 to 48
- key_norm_gain: float32 [128], replicated, may hold values from 0.5 to 1.5
- q_weight: float32 [2048, 2048], P('req', 'mdl'), may hold values from -0.125 to 0.125
- key_matrix: float32 [2048, 1024], P('req', 'mdl'), may hold values from -0.125 to 0.125
- value_matrix: float32 [2048, 1024], P('req', 'mdl'), may hold values from -0.125 to 0.125
- o_weight: float32 [2048, 2048], P('mdl', 'req'), may hold values from -0.125 to 0.125
- gate_weight: float32 [2048, 6144], P('mdl', 'req'), may hold values from -0.125 to 0.125
- up_weight: float32 [2048, 6144], P('mdl', 'req'), may hold values from -0.125 to 0.125
- down_weight: float32 [6144, 2048], P('req', 'mdl'), may hold values from -0.078125 to 0.078125
Outputs:
- layer_out: bfloat16 [16384, 2048], P(('req', 'mdl'))
- key_value_cache: bfloat16 [2, 16384, 1024], P(None, 'req', 'mdl')
Inputs may be any that keep to these rules, and one draw needn't show every extreme that they name: `doc_ids`: A row's prompt number is the index of its prompt's first row among all packed rows, so it never falls along the rows; a prompt holds at most 1024 rows, every aligned block of 1024 rows has a prompt start in its second half, every block but the first begins inside the prompt that the block before it ends with, and the last row starts a prompt. `positions`: positions count from 0 at each prompt's first row.
All inputs are finite; a program needn't handle non-finite values.
Results may differ from a plain program's by a relative error of at most 0.02.
The roundings to bfloat16 on the way count: a program that leaves them out, or rounds other values in their place, can miss the bound.
Values may be sent and summed in bfloat16 or wider, within the bound.
No kernel may reach another device: no remote copies, remote signals or barrier semaphores. Data moves between devices by JAX's collectives and lax.ppermute only.
A program may use at most 128 MiB of HBM per device.

v0:
```python
import math
import jax
import jax.numpy as jnp
from jax import lax
from jax.sharding import PartitionSpec as P

HEAD_SIZE = 128


def passed_along(block, axis, distance):
    devices = range(lax.axis_size(axis))
    route = [(i - distance, i) for i in devices if i - distance in devices]
    return lax.ppermute(block, axis, route)


def root_mean_scale(values, gain):
    return values * lax.rsqrt(jnp.mean(values * values, axis=-1, keepdims=True) + 1e-06) * gain


def apply_rotary(tensor, position):
    half = tensor.shape[-1] // 2
    freq = jnp.exp(
        jnp.arange(half, dtype=jnp.float32) * (-2.0 * math.log(1000000.0) / tensor.shape[-1])
    )
    angle = position.astype(jnp.float32)[:, None] * freq[None, :]
    cosine = jnp.cos(angle)[:, None, :]
    sine = jnp.sin(angle)[:, None, :]
    front = tensor[..., :half]
    back = tensor[..., half:]
    return jnp.concatenate([front * cosine - back * sine, back * cosine + front * sine], axis=-1)


def per_device(
    tokens,
    doc_ids,
    positions,
    attn_gain,
    mlp_gain,
    q_gain,
    key_norm_gain,
    q_weight,
    key_matrix,
    value_matrix,
    o_weight,
    gate_weight,
    up_weight,
    down_weight,
):
    rows_here = tokens.shape[0]
    normed = root_mean_scale(tokens.astype(jnp.float32), attn_gain).astype(jnp.bfloat16)
    query_cols = q_weight.shape[1]
    kv_cols = key_matrix.shape[1]
    pieces = (
        lax.all_gather(q_weight.astype(jnp.bfloat16), "req", axis=0, tiled=True),
        lax.all_gather(key_matrix.astype(jnp.bfloat16), "req", axis=0, tiled=True),
        lax.all_gather(value_matrix.astype(jnp.bfloat16), "req", axis=0, tiled=True),
    )
    query_raw, unnormed_keys, unnormed_values = tuple(
        (jnp.dot(normed, piece, preferred_element_type=jnp.float32) for piece in pieces)
    )
    q_heads = query_cols // HEAD_SIZE
    kv_heads = kv_cols // HEAD_SIZE
    head_groups = q_heads // kv_heads
    query_rows = apply_rotary(
        root_mean_scale(query_raw.reshape(rows_here, q_heads, HEAD_SIZE), q_gain), positions
    ).astype(jnp.bfloat16)
    rotated_keys = (
        apply_rotary(
            root_mean_scale(unnormed_keys.reshape(rows_here, kv_heads, HEAD_SIZE), key_norm_gain),
            positions,
        )
        .astype(jnp.bfloat16)
        .reshape(rows_here, kv_cols)
    )
    projected_values = unnormed_values.astype(jnp.bfloat16)
    key_value_cache = jnp.stack([rotated_keys, projected_values])
    prior_keys, prior_values = passed_along((rotated_keys, projected_values), "req", 1)
    all_keys = jnp.concatenate([prior_keys, rotated_keys], axis=0).reshape(-1, kv_heads, HEAD_SIZE)
    all_values = jnp.concatenate([prior_values, projected_values], axis=0).reshape(
        -1, kv_heads, HEAD_SIZE
    )
    prior_index = jnp.arange(prior_keys.shape[0], dtype=jnp.int32)
    prior_live = prior_index >= rows_here - positions[0]
    grouped_queries = query_rows.reshape(rows_here, kv_heads, head_groups, HEAD_SIZE)
    block_rows = min(512, rows_here)
    scale = HEAD_SIZE ** (-0.5)
    outputs = []
    for block_index in range(rows_here // block_rows):
        lower = block_index * block_rows
        block_q = grouped_queries[lower : lower + block_rows]
        block_doc = doc_ids[lower : lower + block_rows]
        block_pos = positions[lower : lower + block_rows]
        scores = (
            jnp.einsum("qkrd,skd->krqs", block_q, all_keys, preferred_element_type=jnp.float32)
            * scale
        )
        earlier = (block_doc == doc_ids[0])[:, None] & prior_live[None, :]
        current = (doc_ids[None, :] == block_doc[:, None]) & (
            positions[None, :] <= block_pos[:, None]
        )
        allowed = jnp.concatenate([earlier, current], axis=1)
        scores = jnp.where(allowed[None, None], scores, -jnp.inf)
        top = jnp.max(scores, axis=-1, keepdims=True)
        expo = jnp.exp(scores - top)
        probs = (expo / jnp.sum(expo, axis=-1, keepdims=True)).astype(jnp.bfloat16)
        context_block = jnp.einsum(
            "krqs,skd->qkrd", probs, all_values, preferred_element_type=jnp.float32
        )
        outputs.append(context_block.astype(jnp.bfloat16).reshape(block_rows, q_heads * HEAD_SIZE))
    context = jnp.concatenate(outputs, axis=0)
    head_terms = jnp.dot(
        context,
        lax.all_gather(o_weight.astype(jnp.bfloat16), "req", axis=1, tiled=True),
        preferred_element_type=jnp.float32,
    )
    attn_rows = lax.psum_scatter(
        head_terms.astype(jnp.bfloat16), "mdl", scatter_dimension=0, tiled=True
    ).astype(jnp.float32)
    share = rows_here // lax.axis_size("mdl")
    own_rows = lax.dynamic_slice_in_dim(tokens, lax.axis_index("mdl") * share, share, 0)
    resid = lax.optimization_barrier(
        (own_rows.astype(jnp.float32) + attn_rows).astype(jnp.bfloat16)
    ).astype(jnp.float32)
    mlp_in = root_mean_scale(resid, mlp_gain).astype(jnp.bfloat16)
    gate_local = gate_weight.astype(jnp.bfloat16)
    up_local = up_weight.astype(jnp.bfloat16)
    down_local = down_weight.astype(jnp.bfloat16)
    gate_whole, up_whole = (
        lax.all_gather(gate_local, "req", axis=1, tiled=True),
        lax.all_gather(up_local, "req", axis=1, tiled=True),
    )
    down_whole = lax.all_gather(down_local, "req", axis=0, tiled=True)
    gate_server, up_server = (
        lax.all_to_all(gate_whole, "mdl", split_axis=1, concat_axis=0, tiled=True),
        lax.all_to_all(up_whole, "mdl", split_axis=1, concat_axis=0, tiled=True),
    )
    down_server = lax.all_to_all(down_whole, "mdl", split_axis=0, concat_axis=1, tiled=True)
    piece = lax.all_gather(mlp_in, "mdl", axis=0, tiled=True)
    gate = jnp.dot(piece, gate_server, preferred_element_type=jnp.float32)
    upper = jnp.dot(piece, up_server, preferred_element_type=jnp.float32)
    hidden = (jax.nn.silu(gate) * upper).astype(jnp.bfloat16)
    unit_terms = jnp.dot(hidden, down_server, preferred_element_type=jnp.float32)
    mlp_rows = lax.psum_scatter(
        unit_terms.astype(jnp.bfloat16), "mdl", scatter_dimension=0, tiled=True
    ).astype(jnp.float32)
    layer_out = (resid + mlp_rows).astype(jnp.bfloat16)
    return (layer_out, key_value_cache)


def solution(mesh):
    in_specs = (
        P("req", None),
        P("req"),
        P("req"),
        P(),
        P(),
        P(),
        P(),
        P("req", "mdl"),
        P("req", "mdl"),
        P("req", "mdl"),
        P("mdl", "req"),
        P("mdl", "req"),
        P("mdl", "req"),
        P("req", "mdl"),
    )
    out_specs = (P(("req", "mdl"), None), P(None, "req", "mdl"))
    return jax.shard_map(
        per_device, mesh=mesh, in_specs=in_specs, out_specs=out_specs, check_vma=False
    )
```

profile of v0, /device:TPU:1, one launch (start us, length us, event | category | flops | bytes accessed | tf_op | source)
XLA Modules:
  0.0 521.2 jit_solution(16136902884525856238)
XLA Ops:
  10.5 3.2 fusion
  15.0 30.4 %all_gather.25 = bf16[2048,128]{1,0:T(8,128)(2,1)S(1)} all-gather(bf16[128,128]{1,0:T(8,128)(2,1)S(1)} %convert_element_type.105), channel_id=1, replica_groups=mesh['req'=16,'mdl'=8] {'req'}, dimensions={0}, use_global_device_ids=true | all-gather | bytes 557056 | tf_op jit(solution)/shard_map/all_gather | solution.py:55
  53.3 23.4 %all_gather.24 = bf16[2048,128]{1,0:T(8,128)(2,1)S(1)} all-gather(bf16[128,128]{1,0:T(8,128)(2,1)S(1)} %convert_element_type.103), channel_id=1, replica_groups=mesh['req'=16,'mdl'=8] {'req'}, dimensions={0}, use_global_device_ids=true | all-gather | bytes 557056 | tf_op jit(solution)/shard_map/all_gather | solution.py:56
  76.7 4.1 convolution_convert_fusion.2
  80.9 3.5 collective-permute-start
  93.3 4.8 multiply_reduce_fusion
  111.8 3.9 fusion.11
  115.7 3.9 fusion.14
  119.7 4.5 convolution_convert_fusion
  125.9 31.1 %all-gather.13.cloned.1.call-done = bf16[256,6144]{0,1:T(8,128)(2,1)} async-done(((bf16[256,384]{0,1:T(8,128)(2,1)}), bf16[256,6144]{0,1:T(8,128)(2,1)}) %all-gather.13.cloned.1.call-update) | async-done | bytes 3145744 | tf_op jit(solution)/shard_map/all_gather | solution.py:129
  157.0 4.1 all-to-all-start
  161.2 81.4 %reduce-scatter.3.cloned.1.call-done = bf16[128,2048]{1,0:T(8,128)(2,1)} async-done(((bf16[1024,2048]{1,0:T(8,128)(2,1)}), bf16[128,2048]{1,0:T(8,128)(2,1)}) %reduce-scatter.3.cloned.1.call-update) | async-done | bytes 524304 | tf_op jit(solution)/shard_map/reduce_scatter | solution.py:116
  245.7 49.2 %all-gather.15.cloned.1.call-done = bf16[256,6144]{0,1:T(8,128)(2,1)} async-done(((bf16[256,384]{0,1:T(8,128)(2,1)}), bf16[256,6144]{0,1:T(8,128)(2,1)}) %all-gather.15.cloned.1.call-update) | async-done | bytes 3145744 | tf_op jit(solution)/shard_map/all_gather | solution.py:130
  295.0 4.5 all-to-all-start.1
  299.5 54.8 %all-gather.17.cloned.1.call-done = bf16[6144,256]{1,0:T(8,128)(2,1)} async-done(((bf16[384,256]{1,0:T(8,128)(2,1)}), bf16[6144,256]{1,0:T(8,128)(2,1)}) %all-gather.17.cloned.1.call-update) | async-done | bytes 3145744 | tf_op jit(solution)/shard_map/all_gather | solution.py:132
  354.2 4.6 all-to-all-start.2
  358.9 3.1 copy.35
  362.0 3.3 copy.37
  365.2 54.4 %all-to-all-done.2 = bf16[8,768,256]{2,1,0:T(8,128)(2,1)} async-done(((bf16[8,768,256]{2,1,0:T(8,128)(2,1)}), bf16[8,768,256]{2,1,0:T(8,128)(2,1)}, u32[]{:S(2)}, u32[]{:S(2)}) %all-to-all-start.2) | async-done | bytes 3145760 | tf_op jit(solution)/shard_map/all_to_all | solution.py:137
  419.6 4.7 copy.38
  424.3 15.7 %all-gather.11.cloned.1.call-done = bf16[1024,2048]{1,0:T(8,128)(2,1)} async-done(((bf16[128,2048]{1,0:T(8,128)(2,1)}), bf16[1024,2048]{1,0:T(8,128)(2,1)}) %all-gather.11.cloned.1.call-update) | async-done | bytes 4194320 | tf_op jit(solution)/shard_map/all_gather | solution.py:138
  440.0 8.2 %fusion.49 = f32[1024,768]{1,0:T(8,128)} fusion(bf16[1024,2048]{1,0:T(8,128)(2,1)} %all-gather.11.cloned.1.call-done, bf16[2048,768]{1,0:T(8,128)(2,1)} %bitcast.100), kind=kOutput, calls=%fused_computation.91 | convolution fusion | flops 3221225472 | bytes 10485760 | tf_op jit(solution)/shard_map/dot_general | solution.py:139
  448.2 12.2 %convolution_convert_fusion.1 = bf16[1024,2048]{1,0:T(8,128)(2,1)} fusion(bf16[768,2048]{0,1:T(8,128)(2,1)} %bitcast.101, f32[1024,768]{1,0:T(8,128)} %fusion.49, bf16[1024,2048]{1,0:T(8,128)(2,1)} %all-gather.11.cloned.1.call-done, bf16[2048,768]{1,0:T(8,128)(2,1)S(1)} %bitcast.99), kind=kOutput, calls=%fused_computation.22 | convolution fusion | flops 6449266688 | bytes 17825792 | tf_op jit(solution)/shard_map/dot_general | solution.py:142
  463.3 49.1 %reduce-scatter.5.cloned.1.call-done = bf16[128,2048]{1,0:T(8,128)(2,1)} async-done(((bf16[1024,2048]{1,0:T(8,128)(2,1)}), bf16[128,2048]{1,0:T(8,128)(2,1)}) %reduce-scatter.5.cloned.1.call-update) | async-done | bytes 524304 | tf_op jit(solution)/shard_map/reduce_scatter | solution.py:143
  (100 shorter events, 43.8 us)
Async XLA Ops:
  7.2 6.5 %copy-start.10 = (f32[128,128]{1,0:T(8,128)S(1)}, f32[128,128]{1,0:T(8,128)}, u32[]{:S(2)}) copy-start(f32[128,128]{1,0:T(8,128)} %param.22) | copy-start | bytes 196612
  7.2 6.6 %copy-start.14 = (f32[2048]{0:T(1024)S(1)}, f32[2048]{0:T(1024)}, u32[]{:S(2)}) copy-start(f32[2048]{0:T(1024)} %param.17) | copy-start | bytes 24580
  7.2 86.1 %all-gather.7.cloned.1.call-start = ((), (), s32[]{:S(2)}) async-start(), calls=%async_computation.5 | async-start | bytes 1114112 | tf_op jit(solution)/shard_map/all_gather | solution.py:54
  8.8 110.9 %all-gather.9.cloned.1.call-start = ((), (), s32[]{:S(2)}) async-start(), calls=%async_computation.6 | async-start | bytes 1114112 | tf_op jit(solution)/shard_map/all_gather | solution.py:113
  10.4 146.6 %all-gather.13.cloned.1.call-start = ((), (), s32[]{:S(2)}) async-start(), calls=%async_computation.9 | async-start | bytes 3342336 | tf_op jit(solution)/shard_map/all_gather | solution.py:129
  14.9 30.5 %copy-start.1 = (bf16[1024,2048]{1,0:T(8,128)(2,1)}, bf16[1024,2048]{1,0:T(8,128)(2,1)S(1)}, u32[]{:S(2)}) copy-start(bf16[1024,2048]{1,0:T(8,128)(2,1)S(1)} %fusion.2) | copy-start | bytes 12582916
  14.9 32.2 %copy-start.12 = (s32[1024]{0:T(1024)S(1)}, s32[1024]{0:T(1024)}, u32[]{:S(2)}) copy-start(s32[1024]{0:T(1024)} %param.16) | copy-start | bytes 12292
  15.0 32.2 %copy-start.16 = (f32[128]{0:T(128)S(1)}, f32[128]{0:T(128)}, u32[]{:S(2)}) copy-start(f32[128]{0:T(128)} %param.20) | copy-start | bytes 1540
  45.4 7.9 %copy-start.11 = (f32[128,128]{1,0:T(8,128)S(1)}, f32[128,128]{1,0:T(8,128)}, u32[]{:S(2)}) copy-start(f32[128,128]{1,0:T(8,128)} %param.23) | copy-start | bytes 196612
  49.8 34.6 %copy-start.7 = (f32[256,384]{1,0:T(8,128)S(1)}, f32[256,384]{1,0:T(8,128)}, u32[]{:S(2)}) copy-start(f32[256,384]{1,0:T(8,128)} %param.25) | copy-start | bytes 1179652
  50.5 35.0 %copy-start.13 = (s32[1024]{0:T(1024)S(1)}, s32[1024]{0:T(1024)}, u32[]{:S(2)}) copy-start(s32[1024]{0:T(1024)} %param.15) | copy-start | bytes 12292
  51.4 50.4 %collective-permute-start.1 = (bf16[1024,128]{1,0:T(8,128)(2,1)}, bf16[1024,128]{1,0:T(8,128)(2,1)}, u32[]{:S(2)}, u32[]{:S(2)}) collective-permute-start(bf16[1024,128]{1,0:T(8,128)(2,1)} %pad_maximum_fusion.3), channel_id=1, source_target_pairs={{0,8},{8,16},{16,24},{24,32},{32,40},{40,48},{48,56},{56,64},{64,7... | collective-permute-start | bytes 786440 | tf_op jit(solution)/shard_map/ppermute | solution.py:13
  80.9 31.0 %collective-permute-start = (bf16[1024,128]{1,0:T(8,128)(2,1)}, bf16[1024,128]{1,0:T(8,128)(2,1)}, u32[]{:S(2)}, u32[]{:S(2)}) collective-permute-start(bf16[1024,128]{1,0:T(8,128)(2,1)} %convolution_convert_fusion.2), channel_id=1, source_target_pairs={{0,8},{8,16},{16,24},{24,32},{32,40},{40,48},{48,56},{56,64},{64,7... | collective-permute-start | bytes 786440 | tf_op jit(solution)/shard_map/ppermute | solution.py:13
  85.2 157.4 %reduce-scatter.3.cloned.1.call-start = ((), (), s32[]{:S(2)}) async-start(), calls=%async_computation.7 | async-start | bytes 4718592 | tf_op jit(solution)/shard_map/reduce_scatter | solution.py:116
  93.3 6.5 %copy-start.17 = (f32[128]{0:T(128)S(1)}, f32[128]{0:T(128)}, u32[]{:S(2)}) copy-start(f32[128]{0:T(128)} %param.19) | copy-start | bytes 1540
  124.2 170.8 %all-gather.15.cloned.1.call-start = ((), (), s32[]{:S(2)}) async-start(), calls=%async_computation.10 | async-start | bytes 3342336 | tf_op jit(solution)/shard_map/all_gather | solution.py:130
  125.1 229.1 %all-gather.17.cloned.1.call-start = ((), (), s32[]{:S(2)}) async-start(), calls=%async_computation.11 | async-start | bytes 3342336 | tf_op jit(solution)/shard_map/all_gather | solution.py:132
  157.0 87.7 %copy-start.15 = (f32[2048]{0:T(1024)S(1)}, f32[2048]{0:T(1024)}, u32[]{:S(2)}) copy-start(f32[2048]{0:T(1024)} %param.18) | copy-start | bytes 24580
  157.0 138.0 %all-to-all-start = ((bf16[256,8,768]{0,2,1:T(8,128)(2,1)}), bf16[256,8,768]{0,2,1:T(8,128)(2,1)S(1)}, u32[]{:S(2)}, u32[]{:S(2)}) async-start(bf16[256,8,768]{0,2,1:T(8,128)(2,1)} %bitcast.96), calls=%async_computation.1 | async-start | bytes 6291456 | tf_op jit(solution)/shard_map/all_to_all | solution.py:134
  161.2 278.8 %all-gather.11.cloned.1.call-start = ((), (), s32[]{:S(2)}) async-start(), calls=%async_computation.8 | async-start | bytes 4718592 | tf_op jit(solution)/shard_map/all_gather | solution.py:138
  295.0 59.3 %all-to-all-start.1 = ((bf16[256,8,768]{0,2,1:T(8,128)(2,1)}), bf16[256,8,768]{0,2,1:T(8,128)(2,1)}, u32[]{:S(2)}, u32[]{:S(2)}) async-start(bf16[256,8,768]{0,2,1:T(8,128)(2,1)} %bitcast.98), calls=%async_computation.2 | async-start | bytes 6291456 | tf_op jit(solution)/shard_map/all_to_all | solution.py:135
  354.2 65.3 %all-to-all-start.2 = ((bf16[8,768,256]{2,1,0:T(8,128)(2,1)}), bf16[8,768,256]{2,1,0:T(8,128)(2,1)}, u32[]{:S(2)}, u32[]{:S(2)}) async-start(bf16[8,768,256]{2,1,0:T(8,128)(2,1)} %bitcast.97), calls=%async_computation.3 | async-start | bytes 6291456 | tf_op jit(solution)/shard_map/all_to_all | solution.py:137
  358.8 153.6 %reduce-scatter.5.cloned.1.call-start = ((), (), s32[]{:S(2)}) async-start(), calls=%async_computation.12 | async-start | bytes 4718592 | tf_op jit(solution)/shard_map/reduce_scatter | solution.py:143
  460.4 52.0 %copy-start.3 = (bf16[128,2048]{1,0:T(8,128)(2,1)S(1)}, bf16[128,2048]{1,0:T(8,128)(2,1)}, u32[]{:S(2)}) copy-start(bf16[128,2048]{1,0:T(8,128)(2,1)} %copy-done.2) | copy-start | bytes 1572868
  (7 other events, 13.6 us)
Sparse Core Ops, SparseCore 0:
  10.5 48.5 all-gather.6
  61.5 42.2 all-gather.8
  106.2 50.8 all-gather.12
  159.3 83.2 reduce-scatter.2
  244.9 50.0 all-gather.14
  297.3 56.8 all-gather.16
  356.5 83.5 all-gather.10
  460.6 51.7 reduce-scatter.4
where the time goes:
time: 522 us; the launch traced here: 521 us
  waiting for transfers between devices  336 us (64%)
  blocking collectives  53.9 us (10%)
  matrix products  49.1 us (9%)
  other arithmetic  30.2 us (6%)
  starting transfers between devices  19.1 us (4%)
  local copies, waits for them, and re-layouts  17.9 us (3%)
  between operations  15.1 us (3%)
    reduce_scatter x1, waiting for transfers between devices, per_device(): lax.psum_scatter(head_terms.astype(jnp.bfloat16), 'mdl', scatter_dimensio...  81.4 us
    all_gather x1, waiting for transfers between devices, per_device(): down_whole = lax.all_gather(down_local, 'req', axis=0, tiled=True)  54.8 us
    all_to_all x1, waiting for transfers between devices, per_device(): lax.all_to_all(down_whole, 'mdl', split_axis=0, concat_axis=1, tiled=True)  54.4 us
    all_gather x1, waiting for transfers between devices, per_device(): lax.all_gather(up_local, 'req', axis=1, tiled=True)  49.2 us
    reduce_scatter x1, waiting for transfers between devices, per_device(): lax.psum_scatter(unit_terms.astype(jnp.bfloat16), 'mdl', scatter_dimensio...  49.1 us
    all_gather x1, waiting for transfers between devices, per_device(): lax.all_gather(gate_local, 'req', axis=1, tiled=True)  31.1 us
    all_gather x1, blocking collectives, per_device(): lax.all_gather(key_matrix.astype(jnp.bfloat16), 'req', axis=0, tiled=True)  30.4 us
    all_gather x1, blocking collectives, per_device(): lax.all_gather(value_matrix.astype(jnp.bfloat16), 'req', axis=0, tiled=True)  23.4 us
  transfers between devices with their start and end apart: 13, of which 7 were waited for; matrix products, arithmetic and copies ran while one was open for 14% of the time, Pallas kernels for 0%

commit v1 on v0

--- a/solution.py
+++ b/solution.py
@@ -135,7 +135,9 @@
         lax.all_to_all(up_whole, "mdl", split_axis=1, concat_axis=0, tiled=True),
     )
     down_server = lax.all_to_all(down_whole, "mdl", split_axis=0, concat_axis=1, tiled=True)
-    piece = lax.all_gather(mlp_in, "mdl", axis=0, tiled=True)
+    piece = jnp.concatenate(
+        lax.all_to_all(jnp.stack([mlp_in] * lax.axis_size("mdl")), "mdl", 0, 0), axis=0
+    )
     gate = jnp.dot(piece, gate_server, preferred_element_type=jnp.float32)
     upper = jnp.dot(piece, up_server, preferred_element_type=jnp.float32)
     hidden = (jax.nn.silu(gate) * upper).astype(jnp.bfloat16)

time: 522 us -> 503 us (0.964)
  waiting for transfers between devices: 336 us -> 305 us
  local copies, waits for them, and re-layouts: 17.9 us -> 25.1 us
    all_to_all x1, waiting for transfers between devices: 54.4 us -> 0.01 us  [per_device(): lax.all_to_all(down_whole, 'mdl', split_axis=0, concat_axis=1, tiled=True)]
    all_to_all x0 -> x1, waiting for transfers between devices: none -> 37.7 us  [per_device(): lax.all_to_all(jnp.stack([mlp_in] * lax.axis_size('mdl')), 'mdl', 0, 0)]
    all_gather x1 -> x0, waiting for transfers between devices: 15.7 us -> none  [per_device(): piece = lax.all_gather(mlp_in, 'mdl', axis=0, tiled=True)]
    all_gather x1, waiting for transfers between devices: 49.2 us -> 55.2 us  [per_device(): lax.all_gather(up_local, 'req', axis=1, tiled=True)]
  transfers between devices with their start and end apart: 13 -> 13, of which waited for: 7 -> 6; matrix products, arithmetic and copies ran while one was open for 14% -> 15% of each run, Pallas kernels for 0% -> 0%
where the time goes in v1:
time: 503 us; the launch traced here: 502 us
  waiting for transfers between devices  305 us (61%)
  blocking collectives  52.5 us (10%)
  matrix products  49.1 us (10%)
  other arithmetic  31.3 us (6%)
  local copies, waits for them, and re-layouts  25.1 us (5%)
  starting transfers between devices  24 us (5%)
  between operations  15.1 us (3%)
    reduce_scatter x1, waiting for transfers between devices, per_device(): lax.psum_scatter(head_terms.astype(jnp.bfloat16), 'mdl', scatter_dimensio...  81.3 us
    all_gather x1, waiting for transfers between devices, per_device(): lax.all_gather(up_local, 'req', axis=1, tiled=True)  55.2 us
    all_gather x1, waiting for transfers between devices, per_device(): down_whole = lax.all_gather(down_local, 'req', axis=0, tiled=True)  55.1 us
    reduce_scatter x1, waiting for transfers between devices, per_device(): lax.psum_scatter(unit_terms.astype(jnp.bfloat16), 'mdl', scatter_dimensio...  48.7 us
    all_to_all x1, waiting for transfers between devices, per_device(): lax.all_to_all(jnp.stack([mlp_in] * lax.axis_size('mdl')), 'mdl', 0, 0)  37.7 us
    all_gather x1, blocking collectives, per_device(): lax.all_gather(key_matrix.astype(jnp.bfloat16), 'req', axis=0, tiled=True)  29.1 us
    all_gather x1, waiting for transfers between devices, per_device(): lax.all_gather(gate_local, 'req', axis=1, tiled=True)  26.8 us
    all_gather x1, blocking collectives, per_device(): lax.all_gather(value_matrix.astype(jnp.bfloat16), 'req', axis=0, tiled=True)  23.3 us
  transfers between devices with their start and end apart: 13, of which 6 were waited for; matrix products, arithmetic and copies ran while one was open for 15% of the time, Pallas kernels for 0%

profile of v1, /device:TPU:1, one launch (start us, length us, event | category | flops | bytes accessed | tf_op | source)
XLA Modules:
  0.0 502.0 jit_solution(10709741918445854309)
XLA Ops:
  15.2 3.3 fusion
  18.6 29.1 %all_gather.22 = bf16[2048,128]{1,0:T(8,128)(2,1)S(1)} all-gather(bf16[128,128]{1,0:T(8,128)(2,1)S(1)} %convert_element_type.105), channel_id=1, replica_groups=mesh['req'=16,'mdl'=8] {'req'}, dimensions={0}, use_global_device_ids=true | all-gather | bytes 557056 | tf_op jit(solution)/shard_map/all_gather | solution.py:55
  58.6 23.3 %all_gather.21 = bf16[2048,128]{1,0:T(8,128)(2,1)S(1)} all-gather(bf16[128,128]{1,0:T(8,128)(2,1)S(1)} %convert_element_type.103), channel_id=1, replica_groups=mesh['req'=16,'mdl'=8] {'req'}, dimensions={0}, use_global_device_ids=true | all-gather | bytes 557056 | tf_op jit(solution)/shard_map/all_gather | solution.py:56
  81.9 4.1 convolution_convert_fusion.2
  86.1 3.7 collective-permute-start
  98.8 4.8 multiply_reduce_fusion
  117.2 3.9 fusion.11
  121.1 3.9 fusion.14
  125.1 4.5 convolution_convert_fusion
  129.6 26.8 %all-gather.10.cloned.1.call-done = bf16[256,6144]{0,1:T(8,128)(2,1)} async-done(((bf16[256,384]{0,1:T(8,128)(2,1)}), bf16[256,6144]{0,1:T(8,128)(2,1)}) %all-gather.10.cloned.1.call-update) | async-done | bytes 3145744 | tf_op jit(solution)/shard_map/all_gather | solution.py:129
  156.4 4.0 all-to-all-start.1
  160.4 55.2 %all-gather.12.cloned.1.call-done = bf16[256,6144]{0,1:T(8,128)(2,1)} async-done(((bf16[256,384]{0,1:T(8,128)(2,1)}), bf16[256,6144]{0,1:T(8,128)(2,1)}) %all-gather.12.cloned.1.call-update) | async-done | bytes 3145744 | tf_op jit(solution)/shard_map/all_gather | solution.py:130
  215.6 4.6 all-to-all-start.2
  220.2 55.1 %all-gather.14.cloned.1.call-done = bf16[6144,256]{1,0:T(8,128)(2,1)} async-done(((bf16[384,256]{1,0:T(8,128)(2,1)}), bf16[6144,256]{1,0:T(8,128)(2,1)}) %all-gather.14.cloned.1.call-update) | async-done | bytes 3145744 | tf_op jit(solution)/shard_map/all_gather | solution.py:132
  275.3 4.7 all-to-all-start.3
  280.1 81.3 %reduce-scatter.3.cloned.1.call-done = bf16[128,2048]{1,0:T(8,128)(2,1)} async-done(((bf16[1024,2048]{1,0:T(8,128)(2,1)}), bf16[128,2048]{1,0:T(8,128)(2,1)}) %reduce-scatter.3.cloned.1.call-update) | async-done | bytes 524304 | tf_op jit(solution)/shard_map/reduce_scatter | solution.py:116
  364.5 3.5 stack.6
  368.0 4.6 all-to-all-start
  375.7 3.2 copy.37
  378.9 4.7 copy.38
  383.5 37.7 %all-to-all-done = bf16[8,128,2048]{2,1,0:T(8,128)(2,1)} async-done(((bf16[8,128,2048]{2,1,0:T(8,128)(2,1)}), bf16[8,128,2048]{2,1,0:T(8,128)(2,1)}, u32[]{:S(2)}, u32[]{:S(2)}) %all-to-all-start) | async-done | bytes 4194336 | tf_op jit(solution)/shard_map/all_to_all | solution.py:139
  421.2 8.2 %fusion.49 = f32[1024,768]{1,0:T(8,128)} fusion(bf16[1024,2048]{1,0:T(8,128)(2,1)} %bitcast.21, bf16[2048,768]{1,0:T(8,128)(2,1)} %bitcast.101), kind=kOutput, calls=%fused_computation.91 | convolution fusion | flops 3221225472 | bytes 10485760 | tf_op jit(solution)/shard_map/dot_general | solution.py:141
  429.4 12.3 %convolution_convert_fusion.1 = bf16[1024,2048]{1,0:T(8,128)(2,1)} fusion(bf16[768,2048]{0,1:T(8,128)(2,1)} %bitcast.102, f32[1024,768]{1,0:T(8,128)} %fusion.49, bf16[1024,2048]{1,0:T(8,128)(2,1)} %bitcast.21, bf16[2048,768]{1,0:T(8,128)(2,1)S(1)} %bitcast.100), kind=kOutput, calls=%fused_computation.22 | convolution fusion | flops 6449266688 | bytes 17825792 | tf_op jit(solution)/shard_map/dot_general | solution.py:144
  444.6 48.7 %reduce-scatter.5.cloned.1.call-done = bf16[128,2048]{1,0:T(8,128)(2,1)} async-done(((bf16[1024,2048]{1,0:T(8,128)(2,1)}), bf16[128,2048]{1,0:T(8,128)(2,1)}) %reduce-scatter.5.cloned.1.call-update) | async-done | bytes 524304 | tf_op jit(solution)/shard_map/reduce_scatter | solution.py:145
  (94 shorter events, 51.7 us)
Async XLA Ops:
  7.2 40.5 %copy-start.11 = (f32[2048]{0:T(1024)S(1)}, f32[2048]{0:T(1024)}, u32[]{:S(2)}) copy-start(f32[2048]{0:T(1024)} %param.17) | copy-start | bytes 24580
  7.2 91.6 %all-gather.6.cloned.1.call-start = ((), (), s32[]{:S(2)}) async-start(), calls=%async_computation.6 | async-start | bytes 1114112 | tf_op jit(solution)/shard_map/all_gather | solution.py:54
  8.8 116.3 %all-gather.8.cloned.1.call-start = ((), (), s32[]{:S(2)}) async-start(), calls=%async_computation.7 | async-start | bytes 1114112 | tf_op jit(solution)/shard_map/all_gather | solution.py:113
  10.4 146.0 %all-gather.10.cloned.1.call-start = ((), (), s32[]{:S(2)}) async-start(), calls=%async_computation.9 | async-start | bytes 3342336 | tf_op jit(solution)/shard_map/all_gather | solution.py:129
  12.3 203.4 %all-gather.12.cloned.1.call-start = ((), (), s32[]{:S(2)}) async-start(), calls=%async_computation.10 | async-start | bytes 3342336 | tf_op jit(solution)/shard_map/all_gather | solution.py:130
  14.2 261.1 %all-gather.14.cloned.1.call-start = ((), (), s32[]{:S(2)}) async-start(), calls=%async_computation.11 | async-start | bytes 3342336 | tf_op jit(solution)/shard_map/all_gather | solution.py:132
  14.2 33.5 %copy-start = (bf16[1024,2048]{1,0:T(8,128)(2,1)S(1)}, bf16[1024,2048]{1,0:T(8,128)(2,1)}, u32[]{:S(2)}) copy-start(bf16[1024,2048]{1,0:T(8,128)(2,1)} %param.14) | copy-start | bytes 12582916
  48.7 1.9 copy-start.1
  50.7 1.8 copy-start.13
  50.7 7.9 %copy-start.8 = (f32[128,128]{1,0:T(8,128)S(1)}, f32[128,128]{1,0:T(8,128)}, u32[]{:S(2)}) copy-start(f32[128,128]{1,0:T(8,128)} %param.23) | copy-start | bytes 196612
  55.1 34.7 %copy-start.7 = (f32[384,256]{1,0:T(8,128)S(1)}, f32[384,256]{1,0:T(8,128)}, u32[]{:S(2)}) copy-start(f32[384,256]{1,0:T(8,128)} %param.27) | copy-start | bytes 1179652
  55.8 35.0 %copy-start.10 = (s32[1024]{0:T(1024)S(1)}, s32[1024]{0:T(1024)}, u32[]{:S(2)}) copy-start(s32[1024]{0:T(1024)} %param.15) | copy-start | bytes 12292
  56.7 50.5 %collective-permute-start.1 = (bf16[1024,128]{1,0:T(8,128)(2,1)}, bf16[1024,128]{1,0:T(8,128)(2,1)}, u32[]{:S(2)}, u32[]{:S(2)}) collective-permute-start(bf16[1024,128]{1,0:T(8,128)(2,1)} %pad_maximum_fusion.3), channel_id=1, source_target_pairs={{0,8},{8,16},{16,24},{24,32},{32,40},{40,48},{48,56},{56,64},{64,7... | collective-permute-start | bytes 786440 | tf_op jit(solution)/shard_map/ppermute | solution.py:13
  86.1 31.2 %collective-permute-start = (bf16[1024,128]{1,0:T(8,128)(2,1)}, bf16[1024,128]{1,0:T(8,128)(2,1)}, u32[]{:S(2)}, u32[]{:S(2)}) collective-permute-start(bf16[1024,128]{1,0:T(8,128)(2,1)} %convolution_convert_fusion.2), channel_id=1, source_target_pairs={{0,8},{8,16},{16,24},{24,32},{32,40},{40,48},{48,56},{56,64},{64,7... | collective-permute-start | bytes 786440 | tf_op jit(solution)/shard_map/ppermute | solution.py:13
  90.5 270.8 %reduce-scatter.3.cloned.1.call-start = ((), (), s32[]{:S(2)}) async-start(), calls=%async_computation.8 | async-start | bytes 4718592 | tf_op jit(solution)/shard_map/reduce_scatter | solution.py:116
  98.7 6.4 %copy-start.14 = (f32[128]{0:T(128)S(1)}, f32[128]{0:T(128)}, u32[]{:S(2)}) copy-start(f32[128]{0:T(128)} %param.19) | copy-start | bytes 1540
  105.1 2.1 copy-start.5
  156.4 59.3 %all-to-all-start.1 = ((bf16[256,8,768]{0,2,1:T(8,128)(2,1)}), bf16[256,8,768]{0,2,1:T(8,128)(2,1)S(1)}, u32[]{:S(2)}, u32[]{:S(2)}) async-start(bf16[256,8,768]{0,2,1:T(8,128)(2,1)} %bitcast.98), calls=%async_computation.2 | async-start | bytes 6291456 | tf_op jit(solution)/shard_map/all_to_all | solution.py:134
  215.6 59.7 %all-to-all-start.2 = ((bf16[256,8,768]{0,2,1:T(8,128)(2,1)}), bf16[256,8,768]{0,2,1:T(8,128)(2,1)}, u32[]{:S(2)}, u32[]{:S(2)}) async-start(bf16[256,8,768]{0,2,1:T(8,128)(2,1)} %bitcast.97), calls=%async_computation.3 | async-start | bytes 6291456 | tf_op jit(solution)/shard_map/all_to_all | solution.py:135
  275.3 88.1 %copy-start.12 = (f32[2048]{0:T(1024)S(1)}, f32[2048]{0:T(1024)}, u32[]{:S(2)}) copy-start(f32[2048]{0:T(1024)} %param.18) | copy-start | bytes 24580
  275.3 89.1 %all-to-all-start.3 = ((bf16[8,768,256]{2,1,0:T(8,128)(2,1)}), bf16[8,768,256]{2,1,0:T(8,128)(2,1)}, u32[]{:S(2)}, u32[]{:S(2)}) async-start(bf16[8,768,256]{2,1,0:T(8,128)(2,1)} %bitcast.99), calls=%async_computation.4 | async-start | bytes 6291456 | tf_op jit(solution)/shard_map/all_to_all | solution.py:137
  368.0 53.2 %all-to-all-start = ((bf16[8,128,2048]{2,1,0:T(8,128)(2,1)}), bf16[8,128,2048]{2,1,0:T(8,128)(2,1)}, u32[]{:S(2)}, u32[]{:S(2)}) async-start(bf16[8,128,2048]{2,1,0:T(8,128)(2,1)} %stack.6), calls=%async_computation.1 | async-start | bytes 8388608 | tf_op jit(solution)/shard_map/all_to_all | solution.py:139
  372.6 120.7 %reduce-scatter.5.cloned.1.call-start = ((), (), s32[]{:S(2)}) async-start(), calls=%async_computation.12 | async-start | bytes 4718592 | tf_op jit(solution)/shard_map/reduce_scatter | solution.py:145
  441.7 51.5 %copy-start.3 = (bf16[128,2048]{1,0:T(8,128)(2,1)S(1)}, bf16[128,2048]{1,0:T(8,128)(2,1)}, u32[]{:S(2)}) copy-start(bf16[128,2048]{1,0:T(8,128)(2,1)} %copy-done.2) | copy-start | bytes 1572868
  (4 other events, 4.2 us)
Sparse Core Ops, SparseCore 0:
  10.5 48.5 all-gather.5
  61.5 41.5 all-gather.7
  105.6 50.7 all-gather.9
  158.7 56.8 all-gather.11
  217.9 57.3 all-gather.13
  277.6 83.7 reduce-scatter.2
  441.9 51.3 reduce-scatter.4
